TPU v7x, 128 devices: a whole 4x4x4 slice. The times are simulated.
128 devices in a mesh: row: 32 (over x, y, core), col: 4 (over z).
Axes of the slice: x: 4, y: 4, z: 4, core: 2. Of those that a mesh axis runs over, the one named last changes fastest.
Arguments:
- frames: float32 [64, 65536], P(None, ('row', 'col')), may hold values from -8 to 8
- start: float32 [32, 65536], P(None, ('row', 'col')), may hold values from -6 to 6
Outputs:
- basis: float32 [32, 65536], P(None, ('row', 'col'))
All inputs are finite; a program needn't handle non-finite values.
Results may differ from a plain program's by a relative error of at most 0.0003.
Values sent between devices are 32-bit elements; how exact they have to be, the bound alone decides.
A program may use at most 320 MiB of HBM per device.

v0:
```python
import jax
import jax.numpy as jnp
from jax import lax
from jax.sharding import PartitionSpec as P


def build_block(block_points, block_squares, column_points, column_squares):
    products = lax.dot_general(
        block_points, column_points, (((0,), (0,)), ((), ())), precision=lax.Precision.HIGHEST
    )
    distance = block_squares[:, None] + column_squares[None, :] - 2.0 * products
    return jnp.exp(-distance / (0.5 * block_points.shape[0]))


def shards(frames, start):
    block_points = lax.all_gather(frames, "col", axis=1, tiled=True)
    column_points = lax.all_gather(frames, "row", axis=1, tiled=True)
    block_squares = jnp.sum(block_points * block_points, axis=0)
    column_squares = jnp.sum(column_points * column_points, axis=0)
    frame_count = frames.shape[1] * lax.axis_size("row") * lax.axis_size("col")
    block_rows = block_points.shape[1]
    height = min(512, block_rows)
    rounds = block_rows // height

    def kernel_part(index):
        first = index * height
        return build_block(
            block_points[:, first : first + height],
            block_squares[first : first + height],
            column_points,
            column_squares,
        )

    stored = [kernel_part(index) for index in range(rounds)]

    def fetch_tile(index):
        return stored[index]

    def sweep_kernel(spread_weights):
        pieces = []
        for index in range(rounds):
            part = fetch_tile(index)
            if spread_weights is None:
                pieces.append(jnp.sum(part, axis=1)[None, :])
            else:
                pieces.append(
                    lax.dot_general(
                        spread_weights,
                        part,
                        (((1,), (1,)), ((), ())),
                        precision=lax.Precision.HIGHEST,
                    )
                )
        result = jnp.concatenate(pieces, axis=1)
        return result

    def settle(partial_value):
        summed = lax.psum_scatter(partial_value, "col", scatter_dimension=1, tiled=True)
        return summed

    def kernel_product(weights):
        spread_weights = lax.all_gather(weights, "row", axis=1, tiled=True)
        return settle(sweep_kernel(spread_weights))

    def gram_matrix(vectors):
        local_gram = jnp.dot(vectors, vectors.T, precision=lax.Precision.HIGHEST)
        return lax.psum(local_gram, ("row", "col")) / frame_count

    def orthonormal(vectors):
        factor = jnp.linalg.cholesky(gram_matrix(vectors))
        return jax.scipy.linalg.solve_triangular(factor, vectors, lower=True)

    density = settle(sweep_kernel(None))[0]
    inverse = 1.0 / density
    scaled = start * inverse[None, :]
    degree = kernel_product(inverse[None, :])[0]
    product = kernel_product(scaled)
    grown_one = product / degree[None, :]
    basis_one = orthonormal(grown_one)
    grown_two = kernel_product(basis_one * inverse[None, :]) / degree[None, :]
    return orthonormal(grown_two)


def solution(mesh):
    return jax.shard_map(
        shards,
        mesh=mesh,
        in_specs=(P(None, ("row", "col")), P(None, ("row", "col"))),
        out_specs=P(None, ("row", "col")),
        check_vma=False,
    )
```

profile of v0, /device:TPU:1, one launch (start us, length us, event | category | flops | bytes accessed | tf_op | source)
XLA Modules:
  0.0 895.1 jit_solution(2767273097480972749)
XLA Ops:
  6.5 0.7 all-gather.4.cloned.1.call-update
  7.3 13.6 %all_gather.15 = f32[64,2048]{1,0:T(8,128)S(1)} all-gather(f32[64,512]{1,0:T(8,128)} %param.5), channel_id=1, replica_groups=mesh['row'=32,'col'=4] {'col'}, dimensions={1}, use_global_device_ids=true | all-gather | bytes 655360 | tf_op jit(solution)/shard_map/all_gather | solution.py:16
  21.0 38.4 %all-gather.4.cloned.1.call-done = f32[64,16384]{1,0:T(8,128)} async-done(((f32[64,512]{1,0:T(8,128)}), f32[64,16384]{1,0:T(8,128)}) %all-gather.4.cloned.1.call-update) | async-done | bytes 4194320 | tf_op jit(solution)/shard_map/all_gather | solution.py:17
  59.3 2.7 multiply_reduce_fusion
  62.1 37.7 %fusion.27 = (f32[512]{0:T(512)S(1)}, f32[512,16384]{1,0:T(8,128)}) fusion(f32[64,16384]{1,0:T(8,128)} %all-gather.4.cloned.1.call-done, f32[64,2048]{1,0:T(8,128)S(1)} %all_gather.15, f32[16384]{0:T(1024)S(1)} %multiply_reduce_fusion, f32[512]{0:T(512)S(1)} %get-tuple-element.6), kind=kOutput, calls=%fused_computation.53 | convolution fusion | flops 6492782080 | bytes 37949440 | tf_op jit(solution)/shard_map/dot_general | solution.py:8
  99.8 37.0 %fusion.24 = (f32[512]{0:T(512)S(1)}, f32[512,16384]{1,0:T(8,128)}) fusion(f32[64,16384]{1,0:T(8,128)S(1)} %copy-done.2, f32[64,2048]{1,0:T(8,128)S(1)} %all_gather.15, f32[16384]{0:T(1024)S(1)} %multiply_reduce_fusion, f32[512]{0:T(512)S(1)} %get-tuple-element.8), kind=kOutput, calls=%fused_computation.50 | convolution fusion | flops 6492782080 | bytes 37949440 | tf_op jit(solution)/shard_map/dot_general | solution.py:8
  136.8 36.6 %fusion.25 = (f32[512]{0:T(512)S(1)}, f32[512,16384]{1,0:T(8,128)}) fusion(f32[64,16384]{1,0:T(8,128)S(1)} %copy-done.2, f32[64,2048]{1,0:T(8,128)S(1)} %all_gather.15, f32[16384]{0:T(1024)S(1)} %multiply_reduce_fusion, f32[512]{0:T(512)S(1)} %get-tuple-element.9), kind=kOutput, calls=%fused_computation.51 | convolution fusion | flops 6492782080 | bytes 37949440 | tf_op jit(solution)/shard_map/dot_general | solution.py:8
  173.4 36.7 %fusion.26 = (f32[512]{0:T(512)S(1)}, f32[512,16384]{1,0:T(8,128)}) fusion(f32[64,16384]{1,0:T(8,128)S(1)} %copy-done.2, f32[64,2048]{1,0:T(8,128)S(1)} %all_gather.15, f32[16384]{0:T(1024)S(1)} %multiply_reduce_fusion, f32[512]{0:T(512)S(1)} %get-tuple-element.10), kind=kOutput, calls=%fused_computation.52 | convolution fusion | flops 6492782080 | bytes 37949440 | tf_op jit(solution)/shard_map/dot_general | solution.py:8
  210.1 1.4 copy.13
  211.6 21.5 %reduce-scatter.13.cloned.1.call-done = f32[512,1]{1,0:T(8,128)} async-done(((f32[2048,1]{1,0:T(8,128)}), f32[512,1]{1,0:T(8,128)}) %reduce-scatter.13.cloned.1.call-update) | async-done | bytes 2064
  233.0 1.1 copy.14
  234.1 26.0 %all_gather.18 = f32[1,16384]{1,0:T(1,128)S(1)} all-gather(f32[1,512]{1,0:T(1,128)S(1)} %broadcast_divide_fusion.6), channel_id=1, replica_groups=mesh['row'=32,'col'=4] {'row'}, dimensions={1}, use_global_device_ids=true | all-gather | bytes 67584 | tf_op jit(solution)/shard_map/all_gather | solution.py:62
  260.1 0.6 broadcast_multiply_fusion
  260.8 31.2 %fusion.8 = f32[1,512]{1,0:T(1,128)S(1)} fusion(f32[512,16384]{1,0:T(8,128)} %get-tuple-element.16, f32[1,16384]{1,0:T(1,128)S(1)} %all_gather.18), kind=kOutput, calls=%fused_computation.17 | convolution fusion | flops 100663296 | bytes 33622016 | tf_op jit(solution)/shard_map/dot_general | solution.py:47
  292.0 30.9 %fusion.6 = f32[1,512]{1,0:T(1,128)S(1)} fusion(f32[512,16384]{1,0:T(8,128)} %get-tuple-element.14, f32[1,16384]{1,0:T(1,128)S(1)} %all_gather.18), kind=kOutput, calls=%fused_computation.15 | convolution fusion | flops 100663296 | bytes 33622016 | tf_op jit(solution)/shard_map/dot_general | solution.py:47
  322.9 31.0 %fusion.4 = f32[1,512]{1,0:T(1,128)S(1)} fusion(f32[512,16384]{1,0:T(8,128)} %get-tuple-element.12, f32[1,16384]{1,0:T(1,128)S(1)} %all_gather.18), kind=kOutput, calls=%fused_computation.13 | convolution fusion | flops 100663296 | bytes 33622016 | tf_op jit(solution)/shard_map/dot_general | solution.py:47
  353.9 30.8 %fusion.10 = f32[1,512]{1,0:T(1,128)S(1)} fusion(f32[512,16384]{1,0:T(8,128)} %get-tuple-element.18, f32[1,16384]{1,0:T(1,128)S(1)} %all_gather.18), kind=kOutput, calls=%fused_computation.19 | convolution fusion | flops 100663296 | bytes 33622016 | tf_op jit(solution)/shard_map/dot_general | solution.py:47
  384.7 1.4 copy.15
  386.2 34.4 %fusion.31 = f32[32,512]{1,0:T(8,128)S(1)} fusion(f32[32,16384]{1,0:T(8,128)} %all-gather.6.cloned.1.call-done, f32[512,16384]{1,0:T(8,128)} %get-tuple-element.12), kind=kOutput, calls=%fused_computation.57 | convolution fusion | flops 3221225472 | bytes 35717120 | tf_op jit(solution)/shard_map/dot_general | solution.py:47
  420.5 33.9 %fusion.30 = f32[32,512]{1,0:T(8,128)S(1)} fusion(f32[32,16384]{1,0:T(8,128)S(1)} %copy-done, f32[512,16384]{1,0:T(8,128)} %get-tuple-element.14), kind=kOutput, calls=%fused_computation.56 | convolution fusion | flops 3221225472 | bytes 35717120 | tf_op jit(solution)/shard_map/dot_general | solution.py:47
  454.4 34.3 %fusion.29 = f32[32,512]{1,0:T(8,128)S(1)} fusion(f32[32,16384]{1,0:T(8,128)S(1)} %copy-done, f32[512,16384]{1,0:T(8,128)} %get-tuple-element.16), kind=kOutput, calls=%fused_computation.55 | convolution fusion | flops 3221225472 | bytes 35717120 | tf_op jit(solution)/shard_map/dot_general | solution.py:47
  488.8 33.9 %fusion.28 = f32[32,512]{1,0:T(8,128)S(1)} fusion(f32[32,16384]{1,0:T(8,128)S(1)} %copy-done, f32[512,16384]{1,0:T(8,128)} %get-tuple-element.18), kind=kOutput, calls=%fused_computation.54 | convolution fusion | flops 3221225472 | bytes 35717120 | tf_op jit(solution)/shard_map/dot_general | solution.py:47
  522.6 0.7 pad_maximum_fusion
  523.4 1.1 copy.16
  524.5 14.8 %reduce-scatter.9.cloned.1.call-done = f32[32,512]{1,0:T(8,128)} async-done(((f32[32,2048]{1,0:T(8,128)}), f32[32,512]{1,0:T(8,128)}) %reduce-scatter.9.cloned.1.call-update) | async-done | bytes 65552 | tf_op jit(solution)/shard_map/reduce_scatter | solution.py:58
  539.3 1.1 fusion.12
  540.4 67.2 %psum.14 = f32[32,32]{0,1:T(8,128)S(1)} all-reduce(f32[32,32]{0,1:T(8,128)S(1)} %fusion.12), channel_id=1, replica_groups=mesh['row'=32,'col'=4] {'row','col'}, use_global_device_ids=true, to_apply=%region_9.0 | all-reduce | flops 1024 | bytes 8192 | tf_op jit(solution)/shard_map/psum | solution.py:67
  607.6 0.1 copy.8
  607.7 2.9 cholesky.44
  610.6 0.6 compare_reduce_fusion.1
  611.3 0.7 fusion.15
  611.9 2.4 custom-call.6
  614.4 1.8 convolution_multiply_fusion
  616.2 40.7 %all-gather.8.cloned.1.call-done = f32[32,16384]{1,0:T(8,128)} async-done(((f32[32,512]{1,0:T(8,128)}), f32[32,16384]{1,0:T(8,128)}) %all-gather.8.cloned.1.call-update) | async-done | bytes 2097168 | tf_op jit(solution)/shard_map/all_gather | solution.py:62
  656.8 34.2 %fusion.35 = f32[32,512]{1,0:T(8,128)S(1)} fusion(f32[32,16384]{1,0:T(8,128)} %all-gather.8.cloned.1.call-done, f32[512,16384]{1,0:T(8,128)} %get-tuple-element.12), kind=kOutput, calls=%fused_computation.61 | convolution fusion | flops 3221225472 | bytes 35717120 | tf_op jit(solution)/shard_map/dot_general | solution.py:47
  691.0 33.9 %fusion.34 = f32[32,512]{1,0:T(8,128)S(1)} fusion(f32[32,16384]{1,0:T(8,128)S(1)} %copy-done.1, f32[512,16384]{1,0:T(8,128)} %get-tuple-element.14), kind=kOutput, calls=%fused_computation.60 | convolution fusion | flops 3221225472 | bytes 35717120 | tf_op jit(solution)/shard_map/dot_general | solution.py:47
  724.9 34.1 %fusion.33 = f32[32,512]{1,0:T(8,128)S(1)} fusion(f32[32,16384]{1,0:T(8,128)S(1)} %copy-done.1, f32[512,16384]{1,0:T(8,128)} %get-tuple-element.16), kind=kOutput, calls=%fused_computation.59 | convolution fusion | flops 3221225472 | bytes 35717120 | tf_op jit(solution)/shard_map/dot_general | solution.py:47
  759.0 33.9 %fusion.32 = f32[32,512]{1,0:T(8,128)S(1)} fusion(f32[32,16384]{1,0:T(8,128)S(1)} %copy-done.1, f32[512,16384]{1,0:T(8,128)} %get-tuple-element.18), kind=kOutput, calls=%fused_computation.58 | convolution fusion | flops 3221225472 | bytes 35717120 | tf_op jit(solution)/shard_map/dot_general | solution.py:47
  792.9 0.7 pad_maximum_fusion.1
  793.6 17.6 %reduce-scatter.11.cloned.1.call-done = f32[32,512]{1,0:T(8,128)} async-done(((f32[32,2048]{1,0:T(8,128)}), f32[32,512]{1,0:T(8,128)}) %reduce-scatter.11.cloned.1.call-update) | async-done | bytes 65552 | tf_op jit(solution)/shard_map/reduce_scatter | solution.py:58
  811.2 1.1 fusion.14
  812.3 67.0 %psum.15 = f32[32,32]{0,1:T(8,128)S(1)} all-reduce(f32[32,32]{0,1:T(8,128)S(1)} %fusion.14), channel_id=1, replica_groups=mesh['row'=32,'col'=4] {'row','col'}, use_global_device_ids=true, to_apply=%region_13.16 | all-reduce | flops 1024 | bytes 8192 | tf_op jit(solution)/shard_map/psum | solution.py:67
  879.3 0.1 copy.10
  879.4 2.9 cholesky.55
  882.4 0.6 compare_reduce_fusion
  883.0 0.7 fusion.16
  883.7 2.4 custom-call.7
  886.1 1.8 fusion.13
  (34 shorter events, 0.6 us)
Async XLA Ops:
  6.5 52.8 %all-gather.4.cloned.1.call-start = ((), (), s32[]{:S(2)}) async-start(), calls=%async_computation.4 | async-start | bytes 4325376 | tf_op jit(solution)/shard_map/all_gather | solution.py:17
  7.3 225.8 %reduce-scatter.13.cloned.1.call-start = ((), (), s32[]{:S(2)}) async-start(), calls=%async_computation.9 | async-start | bytes 1310720
  59.3 40.5 %copy-start.2 = (f32[64,16384]{1,0:T(8,128)S(1)}, f32[64,16384]{1,0:T(8,128)}, u32[]{:S(2)}) copy-start(f32[64,16384]{1,0:T(8,128)} %all-gather.4.cloned.1.call-done) | copy-start | bytes 12582916
  173.4 86.7 %copy-start.3 = (f32[32,512]{1,0:T(8,128)S(1)}, f32[32,512]{1,0:T(8,128)}, u32[]{:S(2)}) copy-start(f32[32,512]{1,0:T(8,128)} %param.6) | copy-start | bytes 196612
  211.5 174.6 %all-gather.6.cloned.1.call-start = ((), (), s32[]{:S(2)}) async-start(), calls=%async_computation.5 | async-start | bytes 2162688 | tf_op jit(solution)/shard_map/all_gather | solution.py:62
  260.8 262.7 %reduce-scatter.15.cloned.1.call-start = ((), (), s32[]{:S(2)}) async-start(), calls=%async_computation.10 | async-start | bytes 1310720
  386.1 153.2 %reduce-scatter.9.cloned.1.call-start = ((), (), s32[]{:S(2)}) async-start(), calls=%async_computation.6 | async-start | bytes 327680 | tf_op jit(solution)/shard_map/reduce_scatter | solution.py:58
  386.1 34.4 %copy-start = (f32[32,16384]{1,0:T(8,128)S(1)}, f32[32,16384]{1,0:T(8,128)}, u32[]{:S(2)}) copy-start(f32[32,16384]{1,0:T(8,128)} %all-gather.6.cloned.1.call-done) | copy-start | bytes 6291460
  523.4 133.5 %all-gather.8.cloned.1.call-start = ((), (), s32[]{:S(2)}) async-start(), calls=%async_computation.7 | async-start | bytes 2162688 | tf_op jit(solution)/shard_map/all_gather | solution.py:62
  616.1 195.1 %reduce-scatter.11.cloned.1.call-start = ((), (), s32[]{:S(2)}) async-start(), calls=%async_computation.8 | async-start | bytes 327680 | tf_op jit(solution)/shard_map/reduce_scatter | solution.py:58
  656.8 34.2 %copy-start.1 = (f32[32,16384]{1,0:T(8,128)S(1)}, f32[32,16384]{1,0:T(8,128)}, u32[]{:S(2)}) copy-start(f32[32,16384]{1,0:T(8,128)} %all-gather.8.cloned.1.call-done) | copy-start | bytes 6291460
Sparse Core Ops, SparseCore 0:
  9.7 49.5 all-gather.3
  211.6 21.3 reduce-scatter.12
  260.9 41.3 all-gather.5
  386.2 19.1 reduce-scatter.14
  523.5 15.7 reduce-scatter.8
  616.3 40.5 all-gather.7
  793.7 17.4 reduce-scatter.10
where the time goes:
time: 902 us; the launch traced here: 895 us
  matrix products  550 us (61%)
  blocking collectives  174 us (19%)
  waiting for transfers between devices  134 us (15%)
  other arithmetic  18.3 us (2%)
  between operations  14 us (2%)
    dot_general x12, matrix products, sweep_kernel(): lax.dot_general(spread_weights, part, (((1,), (1,)), ((), ())), precision...  396 us
    dot_general x4, matrix products, build_block(): lax.dot_general(block_points, column_points, (((0,), (0,)), ((), ())), pr...  148 us
    psum x2, blocking collectives, gram_matrix(): return lax.psum(local_gram, ('row', 'col')) / frame_count  134 us
    all_gather x2, waiting for transfers between devices, kernel_product(): spread_weights = lax.all_gather(weights, 'row', axis=1, tiled=True)  40.7 us
    all_gather x1, waiting for transfers between devices, shards(): column_points = lax.all_gather(frames, 'row', axis=1, tiled=True)  38.4 us
    reduce_scatter x2, waiting for transfers between devices, settle(): lax.psum_scatter(partial_value, 'col', scatter_dimension=1, tiled=True)  32.4 us
    all_gather x1, blocking collectives, kernel_product(): spread_weights = lax.all_gather(weights, 'row', axis=1, tiled=True)  26 us
    unnamed x9, waiting for transfers between devices  22.3 us
  transfers between devices with their start and end apart: 7, of which 5 were waited for; matrix products, arithmetic and copies ran while one was open for 29% of the time, Pallas kernels for 0%

commit v1 on v0

--- a/solution.py
+++ b/solution.py
@@ -64,7 +64,7 @@
 
     def gram_matrix(vectors):
         local_gram = jnp.dot(vectors, vectors.T, precision=lax.Precision.HIGHEST)
-        return lax.psum(local_gram, ("row", "col")) / frame_count
+        return lax.psum(lax.psum(local_gram, "row"), "col") / frame_count
 
     def orthonormal(vectors):
         factor = jnp.linalg.cholesky(gram_matrix(vectors))

time: 902 us -> 1050 us (1.16)
  blocking collectives: 174 us -> 310 us
    psum x2 -> x4, blocking collectives: 134 us -> 270 us  [gram_matrix(): return lax.psum(lax.psum(local_gram, 'row'), 'col') / frame_count]
  transfers between devices with their start and end apart: 7 -> 7, of which waited for: 5 -> 5; matrix products, arithmetic and copies ran while one was open for 29% -> 25% of each run, Pallas kernels for 0% -> 0%
where the time goes in v1:
time: 1050 us; the launch traced here: 1040 us
  matrix products  550 us (52%)
  blocking collectives  310 us (30%)
  waiting for transfers between devices  140 us (13%)
  other arithmetic  18.3 us (2%)
  between operations  13.9 us (1%)
    dot_general x12, matrix products, sweep_kernel(): lax.dot_general(spread_weights, part, (((1,), (1,)), ((), ())), precision...  396 us
    psum x4, blocking collectives, gram_matrix(): return lax.psum(lax.psum(local_gram, 'row'), 'col') / frame_count  270 us
    dot_general x4, matrix products, build_block(): lax.dot_general(block_points, column_points, (((0,), (0,)), ((), ())), pr...  148 us
    all_gather x2, waiting for transfers between devices, kernel_product(): spread_weights = lax.all_gather(weights, 'row', axis=1, tiled=True)  46.8 us
    all_gather x1, waiting for transfers between devices, shards(): column_points = lax.all_gather(frames, 'row', axis=1, tiled=True)  38.4 us
    reduce_scatter x2, waiting for transfers between devices, settle(): lax.psum_scatter(partial_value, 'col', scatter_dimension=1, tiled=True)  32.4 us
    all_gather x1, blocking collectives, kernel_product(): spread_weights = lax.all_gather(weights, 'row', axis=1, tiled=True)  26 us
    unnamed x9, waiting for transfers between devices  22.3 us
  transfers between devices with their start and end apart: 7, of which 5 were waited for; matrix products, arithmetic and copies ran while one was open for 25% of the time, Pallas kernels for 0%

profile of v1, /device:TPU:1, one launch (start us, length us, event | category | flops | bytes accessed | tf_op | source)
XLA Modules:
  0.0 1037.3 jit_solution(17485279369941070433)
XLA Ops:
  6.5 0.7 all-gather.4.cloned.1.call-update
  7.3 13.6 %all_gather.15 = f32[64,2048]{1,0:T(8,128)S(1)} all-gather(f32[64,512]{1,0:T(8,128)} %param.5), channel_id=1, replica_groups=mesh['row'=32,'col'=4] {'col'}, dimensions={1}, use_global_device_ids=true | all-gather | bytes 655360 | tf_op jit(solution)/shard_map/all_gather | solution.py:16
  21.0 38.4 %all-gather.4.cloned.1.call-done = f32[64,16384]{1,0:T(8,128)} async-done(((f32[64,512]{1,0:T(8,128)}), f32[64,16384]{1,0:T(8,128)}) %all-gather.4.cloned.1.call-update) | async-done | bytes 4194320 | tf_op jit(solution)/shard_map/all_gather | solution.py:17
  59.3 2.7 multiply_reduce_fusion
  62.1 37.7 %fusion.27 = (f32[512]{0:T(512)S(1)}, f32[512,16384]{1,0:T(8,128)}) fusion(f32[64,16384]{1,0:T(8,128)} %all-gather.4.cloned.1.call-done, f32[64,2048]{1,0:T(8,128)S(1)} %all_gather.15, f32[16384]{0:T(1024)S(1)} %multiply_reduce_fusion, f32[512]{0:T(512)S(1)} %get-tuple-element.6), kind=kOutput, calls=%fused_computation.53 | convolution fusion | flops 6492782080 | bytes 37949440 | tf_op jit(solution)/shard_map/dot_general | solution.py:8
  99.8 37.0 %fusion.24 = (f32[512]{0:T(512)S(1)}, f32[512,16384]{1,0:T(8,128)}) fusion(f32[64,16384]{1,0:T(8,128)S(1)} %copy-done.2, f32[64,2048]{1,0:T(8,128)S(1)} %all_gather.15, f32[16384]{0:T(1024)S(1)} %multiply_reduce_fusion, f32[512]{0:T(512)S(1)} %get-tuple-element.8), kind=kOutput, calls=%fused_computation.50 | convolution fusion | flops 6492782080 | bytes 37949440 | tf_op jit(solution)/shard_map/dot_general | solution.py:8
  136.8 36.6 %fusion.25 = (f32[512]{0:T(512)S(1)}, f32[512,16384]{1,0:T(8,128)}) fusion(f32[64,16384]{1,0:T(8,128)S(1)} %copy-done.2, f32[64,2048]{1,0:T(8,128)S(1)} %all_gather.15, f32[16384]{0:T(1024)S(1)} %multiply_reduce_fusion, f32[512]{0:T(512)S(1)} %get-tuple-element.9), kind=kOutput, calls=%fused_computation.51 | convolution fusion | flops 6492782080 | bytes 37949440 | tf_op jit(solution)/shard_map/dot_general | solution.py:8
  173.4 36.7 %fusion.26 = (f32[512]{0:T(512)S(1)}, f32[512,16384]{1,0:T(8,128)}) fusion(f32[64,16384]{1,0:T(8,128)S(1)} %copy-done.2, f32[64,2048]{1,0:T(8,128)S(1)} %all_gather.15, f32[16384]{0:T(1024)S(1)} %multiply_reduce_fusion, f32[512]{0:T(512)S(1)} %get-tuple-element.10), kind=kOutput, calls=%fused_computation.52 | convolution fusion | flops 6492782080 | bytes 37949440 | tf_op jit(solution)/shard_map/dot_general | solution.py:8
  210.1 1.4 copy.13
  211.6 21.5 %reduce-scatter.13.cloned.1.call-done = f32[512,1]{1,0:T(8,128)} async-done(((f32[2048,1]{1,0:T(8,128)}), f32[512,1]{1,0:T(8,128)}) %reduce-scatter.13.cloned.1.call-update) | async-done | bytes 2064
  233.0 1.1 copy.14
  234.1 26.0 %all_gather.18 = f32[1,16384]{1,0:T(1,128)S(1)} all-gather(f32[1,512]{1,0:T(1,128)S(1)} %broadcast_divide_fusion.6), channel_id=1, replica_groups=mesh['row'=32,'col'=4] {'row'}, dimensions={1}, use_global_device_ids=true | all-gather | bytes 67584 | tf_op jit(solution)/shard_map/all_gather | solution.py:62
  260.1 0.6 broadcast_multiply_fusion
  260.8 31.2 %fusion.8 = f32[1,512]{1,0:T(1,128)S(1)} fusion(f32[512,16384]{1,0:T(8,128)} %get-tuple-element.16, f32[1,16384]{1,0:T(1,128)S(1)} %all_gather.18), kind=kOutput, calls=%fused_computation.17 | convolution fusion | flops 100663296 | bytes 33622016 | tf_op jit(solution)/shard_map/dot_general | solution.py:47
  292.0 30.9 %fusion.6 = f32[1,512]{1,0:T(1,128)S(1)} fusion(f32[512,16384]{1,0:T(8,128)} %get-tuple-element.14, f32[1,16384]{1,0:T(1,128)S(1)} %all_gather.18), kind=kOutput, calls=%fused_computation.15 | convolution fusion | flops 100663296 | bytes 33622016 | tf_op jit(solution)/shard_map/dot_general | solution.py:47
  322.9 31.0 %fusion.4 = f32[1,512]{1,0:T(1,128)S(1)} fusion(f32[512,16384]{1,0:T(8,128)} %get-tuple-element.12, f32[1,16384]{1,0:T(1,128)S(1)} %all_gather.18), kind=kOutput, calls=%fused_computation.13 | convolution fusion | flops 100663296 | bytes 33622016 | tf_op jit(solution)/shard_map/dot_general | solution.py:47
  353.9 30.8 %fusion.10 = f32[1,512]{1,0:T(1,128)S(1)} fusion(f32[512,16384]{1,0:T(8,128)} %get-tuple-element.18, f32[1,16384]{1,0:T(1,128)S(1)} %all_gather.18), kind=kOutput, calls=%fused_computation.19 | convolution fusion | flops 100663296 | bytes 33622016 | tf_op jit(solution)/shard_map/dot_general | solution.py:47
  384.7 1.4 copy.15
  386.2 34.4 %fusion.31 = f32[32,512]{1,0:T(8,128)S(1)} fusion(f32[32,16384]{1,0:T(8,128)} %all-gather.6.cloned.1.call-done, f32[512,16384]{1,0:T(8,128)} %get-tuple-element.12), kind=kOutput, calls=%fused_computation.57 | convolution fusion | flops 3221225472 | bytes 35717120 | tf_op jit(solution)/shard_map/dot_general | solution.py:47
  420.5 33.9 %fusion.30 = f32[32,512]{1,0:T(8,128)S(1)} fusion(f32[32,16384]{1,0:T(8,128)S(1)} %copy-done, f32[512,16384]{1,0:T(8,128)} %get-tuple-element.14), kind=kOutput, calls=%fused_computation.56 | convolution fusion | flops 3221225472 | bytes 35717120 | tf_op jit(solution)/shard_map/dot_general | solution.py:47
  454.4 34.3 %fusion.29 = f32[32,512]{1,0:T(8,128)S(1)} fusion(f32[32,16384]{1,0:T(8,128)S(1)} %copy-done, f32[512,16384]{1,0:T(8,128)} %get-tuple-element.16), kind=kOutput, calls=%fused_computation.55 | convolution fusion | flops 3221225472 | bytes 35717120 | tf_op jit(solution)/shard_map/dot_general | solution.py:47
  488.8 33.9 %fusion.28 = f32[32,512]{1,0:T(8,128)S(1)} fusion(f32[32,16384]{1,0:T(8,128)S(1)} %copy-done, f32[512,16384]{1,0:T(8,128)} %get-tuple-element.18), kind=kOutput, calls=%fused_computation.54 | convolution fusion | flops 3221225472 | bytes 35717120 | tf_op jit(solution)/shard_map/dot_general | solution.py:47
  522.6 0.7 pad_maximum_fusion
  523.4 1.1 copy.16
  524.5 14.8 %reduce-scatter.9.cloned.1.call-done = f32[32,512]{1,0:T(8,128)} async-done(((f32[32,2048]{1,0:T(8,128)}), f32[32,512]{1,0:T(8,128)}) %reduce-scatter.9.cloned.1.call-update) | async-done | bytes 65552 | tf_op jit(solution)/shard_map/reduce_scatter | solution.py:58
  539.3 1.1 fusion.12
  540.4 123.2 %psum.28 = f32[32,32]{0,1:T(8,128)S(1)} all-reduce(f32[32,32]{0,1:T(8,128)S(1)} %fusion.12), channel_id=1, replica_groups=mesh['row'=32,'col'=4] {'row'}, use_global_device_ids=true, to_apply=%region_9.0 | all-reduce | flops 1024 | bytes 8192 | tf_op jit(solution)/shard_map/psum | solution.py:67
  663.7 12.0 %psum.29 = f32[32,32]{0,1:T(8,128)S(1)} all-reduce(f32[32,32]{0,1:T(8,128)S(1)} %psum.28), channel_id=1, replica_groups=mesh['row'=32,'col'=4] {'col'}, use_global_device_ids=true, to_apply=%region_10.0 | all-reduce | flops 1024 | bytes 8192 | tf_op jit(solution)/shard_map/psum | solution.py:67
  675.8 2.9 cholesky.44
  678.7 0.6 compare_reduce_fusion.1
  679.4 0.7 fusion.15
  680.0 2.4 custom-call.6
  682.5 1.8 convolution_multiply_fusion
  684.3 46.8 %all-gather.8.cloned.1.call-done = f32[32,16384]{1,0:T(8,128)} async-done(((f32[32,512]{1,0:T(8,128)}), f32[32,16384]{1,0:T(8,128)}) %all-gather.8.cloned.1.call-update) | async-done | bytes 2097168 | tf_op jit(solution)/shard_map/all_gather | solution.py:62
  731.1 34.2 %fusion.35 = f32[32,512]{1,0:T(8,128)S(1)} fusion(f32[32,16384]{1,0:T(8,128)} %all-gather.8.cloned.1.call-done, f32[512,16384]{1,0:T(8,128)} %get-tuple-element.12), kind=kOutput, calls=%fused_computation.61 | convolution fusion | flops 3221225472 | bytes 35717120 | tf_op jit(solution)/shard_map/dot_general | solution.py:47
  765.3 33.9 %fusion.34 = f32[32,512]{1,0:T(8,128)S(1)} fusion(f32[32,16384]{1,0:T(8,128)S(1)} %copy-done.1, f32[512,16384]{1,0:T(8,128)} %get-tuple-element.14), kind=kOutput, calls=%fused_computation.60 | convolution fusion | flops 3221225472 | bytes 35717120 | tf_op jit(solution)/shard_map/dot_general | solution.py:47
  799.2 34.1 %fusion.33 = f32[32,512]{1,0:T(8,128)S(1)} fusion(f32[32,16384]{1,0:T(8,128)S(1)} %copy-done.1, f32[512,16384]{1,0:T(8,128)} %get-tuple-element.16), kind=kOutput, calls=%fused_computation.59 | convolution fusion | flops 3221225472 | bytes 35717120 | tf_op jit(solution)/shard_map/dot_general | solution.py:47
  833.3 33.9 %fusion.32 = f32[32,512]{1,0:T(8,128)S(1)} fusion(f32[32,16384]{1,0:T(8,128)S(1)} %copy-done.1, f32[512,16384]{1,0:T(8,128)} %get-tuple-element.18), kind=kOutput, calls=%fused_computation.58 | convolution fusion | flops 3221225472 | bytes 35717120 | tf_op jit(solution)/shard_map/dot_general | solution.py:47
  867.2 0.7 pad_maximum_fusion.1
  867.9 17.6 %reduce-scatter.11.cloned.1.call-done = f32[32,512]{1,0:T(8,128)} async-done(((f32[32,2048]{1,0:T(8,128)}), f32[32,512]{1,0:T(8,128)}) %reduce-scatter.11.cloned.1.call-update) | async-done | bytes 65552 | tf_op jit(solution)/shard_map/reduce_scatter | solution.py:58
  885.5 1.1 fusion.14
  886.6 123.0 %psum.30 = f32[32,32]{0,1:T(8,128)S(1)} all-reduce(f32[32,32]{0,1:T(8,128)S(1)} %fusion.14), channel_id=1, replica_groups=mesh['row'=32,'col'=4] {'row'}, use_global_device_ids=true, to_apply=%region_14.17 | all-reduce | flops 1024 | bytes 8192 | tf_op jit(solution)/shard_map/psum | solution.py:67
  1009.7 12.0 %psum.31 = f32[32,32]{0,1:T(8,128)S(1)} all-reduce(f32[32,32]{0,1:T(8,128)S(1)} %psum.30), channel_id=1, replica_groups=mesh['row'=32,'col'=4] {'col'}, use_global_device_ids=true, to_apply=%region_15.18 | all-reduce | flops 1024 | bytes 8192 | tf_op jit(solution)/shard_map/psum | solution.py:67
  1021.8 2.9 cholesky.55
  1024.7 0.6 compare_reduce_fusion
  1025.4 0.7 fusion.16
  1026.1 2.4 custom-call.7
  1028.5 1.7 fusion.13
  (36 shorter events, 0.7 us)
Async XLA Ops:
  6.5 52.8 %all-gather.4.cloned.1.call-start = ((), (), s32[]{:S(2)}) async-start(), calls=%async_computation.4 | async-start | bytes 4325376 | tf_op jit(solution)/shard_map/all_gather | solution.py:17
  7.3 225.8 %reduce-scatter.13.cloned.1.call-start = ((), (), s32[]{:S(2)}) async-start(), calls=%async_computation.9 | async-start | bytes 1310720
  59.3 40.5 %copy-start.2 = (f32[64,16384]{1,0:T(8,128)S(1)}, f32[64,16384]{1,0:T(8,128)}, u32[]{:S(2)}) copy-start(f32[64,16384]{1,0:T(8,128)} %all-gather.4.cloned.1.call-done) | copy-start | bytes 12582916
  173.4 86.7 %copy-start.3 = (f32[32,512]{1,0:T(8,128)S(1)}, f32[32,512]{1,0:T(8,128)}, u32[]{:S(2)}) copy-start(f32[32,512]{1,0:T(8,128)} %param.6) | copy-start | bytes 196612
  211.5 174.6 %all-gather.6.cloned.1.call-start = ((), (), s32[]{:S(2)}) async-start(), calls=%async_computation.5 | async-start | bytes 2162688 | tf_op jit(solution)/shard_map/all_gather | solution.py:62
  260.8 262.7 %reduce-scatter.15.cloned.1.call-start = ((), (), s32[]{:S(2)}) async-start(), calls=%async_computation.10 | async-start | bytes 1310720
  386.1 153.2 %reduce-scatter.9.cloned.1.call-start = ((), (), s32[]{:S(2)}) async-start(), calls=%async_computation.6 | async-start | bytes 327680 | tf_op jit(solution)/shard_map/reduce_scatter | solution.py:58
  386.1 34.4 %copy-start = (f32[32,16384]{1,0:T(8,128)S(1)}, f32[32,16384]{1,0:T(8,128)}, u32[]{:S(2)}) copy-start(f32[32,16384]{1,0:T(8,128)} %all-gather.6.cloned.1.call-done) | copy-start | bytes 6291460
  523.4 207.8 %all-gather.8.cloned.1.call-start = ((), (), s32[]{:S(2)}) async-start(), calls=%async_computation.7 | async-start | bytes 2162688 | tf_op jit(solution)/shard_map/all_gather | solution.py:62
  684.2 201.3 %reduce-scatter.11.cloned.1.call-start = ((), (), s32[]{:S(2)}) async-start(), calls=%async_computation.8 | async-start | bytes 327680 | tf_op jit(solution)/shard_map/reduce_scatter | solution.py:58
  731.1 34.2 %copy-start.1 = (f32[32,16384]{1,0:T(8,128)S(1)}, f32[32,16384]{1,0:T(8,128)}, u32[]{:S(2)}) copy-start(f32[32,16384]{1,0:T(8,128)} %all-gather.8.cloned.1.call-done) | copy-start | bytes 6291460
Sparse Core Ops, SparseCore 0:
  9.7 49.5 all-gather.3
  211.6 21.3 reduce-scatter.12
  260.9 41.3 all-gather.5
  386.2 19.1 reduce-scatter.14
  523.5 15.7 reduce-scatter.8
  684.4 46.7 all-gather.7
  868.0 17.4 reduce-scatter.10
